TPU v7x, 32 devices: a whole 2x2x4 slice. The times are simulated.
32 devices in a mesh: mesh: 32 (over z, y, x, core).
Axes of the slice: x: 2, y: 2, z: 4, core: 2. Of those that a mesh axis runs over, the one named last changes fastest.
Arguments:
- states: float32 [196608, 256], P('mesh'), may hold values from -30 to 30
- inv_sqrt_mass: float32 [196608], P('mesh'), may hold values from 0.25 to 1.75
- element_blocks: bfloat16 [512, 512, 512], P('mesh'), may hold values from -0.25 to 0.25
- element_nodes: int32 [512, 512], P('mesh'), may hold values from 0 to 6143, as said below
- element_counts: int32 [32], P('mesh'), may hold values from 1 to 16, as said below
- node_counts: int32 [32], replicated, may hold values from 4608 to 6144, as said below
- boundary_rows: int32 [32, 2, 384], P('mesh'), may hold values from 0 to 4607, as said below
Outputs:
- rotated: float32 [196608, 256], P('mesh')
Inputs may be any that keep to these rules, and one draw needn't show every extreme that they name: `node_counts`: live node rows of each device; some device has 6144. `element_counts`: live element slots of each device (the first slots are live); some device has 16. `element_nodes`: every entry is below its device's node count. `boundary_rows`: for each device the 768 entries are distinct rows below 4608.
All inputs are finite; a program needn't handle non-finite values.
Results may differ from a plain program's by a relative error of at most 0.0077.
Values sent between devices are 32-bit elements; how exact they have to be, the bound alone decides.
A program may use at most 128 MiB of HBM per device.

v0:
```python
import jax
import jax.numpy as jnp
from jax import lax
from jax.sharding import PartitionSpec as P


def passed_along(block, axis, distance):
    devices = range(lax.axis_size(axis))
    route = [(i - distance, i) for i in devices if i - distance in devices]
    return lax.ppermute(block, axis, route)


def body(
    states, inv_sqrt_mass, element_blocks, element_nodes, element_counts, node_counts, boundary_rows
):
    position = lax.axis_index("mesh")
    devices = lax.axis_size("mesh")
    row_total = states.shape[0]
    width = states.shape[1]
    slots = element_blocks.shape[0]
    lower_rows = boundary_rows[0, 0]
    upper_rows = boundary_rows[0, 1]
    shared = lower_rows.shape[0]
    has_below = position >= 1
    owner_vals, owner_mass = passed_along(
        (states[upper_rows], inv_sqrt_mass[upper_rows]), "mesh", 1
    )
    field = states.at[lower_rows].set(jnp.where(has_below, owner_vals, states[lower_rows]))
    mass = inv_sqrt_mass.at[lower_rows].set(
        jnp.where(has_below, owner_mass, inv_sqrt_mass[lower_rows])
    )
    live_slots = element_counts[0]
    row_index = jnp.arange(row_total)
    slot_index = jnp.arange(slots)
    slot_live = slot_index < live_slots

    def ham(values):
        scaled = (mass[:, None] * values).astype(jnp.bfloat16)
        empty = jnp.zeros((row_total, width), jnp.float32)

        def add_element(slot, total):
            rows = element_nodes[slot]

            def compute(acc):
                part = jnp.dot(
                    element_blocks[slot], scaled[rows], preferred_element_type=jnp.float32
                )
                return acc.at[rows].add(part)

            return lax.cond(slot_live[slot], compute, lambda acc: acc, total)

        local = lax.fori_loop(0, slots, add_element, empty)
        coming_up = passed_along(local[upper_rows], "mesh", 1)
        coming_down = passed_along(local[lower_rows], "mesh", -1)
        assembled = local.at[lower_rows].add(coming_up).at[upper_rows].add(coming_down)
        return mass[:, None] * assembled

    center = 0.5
    half_width = 1.5
    first = (ham(field) - center * field) / half_width
    second = 2.0 * (ham(first) - center * first) / half_width - field
    filtered = 2.0 * (ham(second) - center * second) / half_width - first
    live = row_index < node_counts[position]
    in_lower = jnp.any(row_index[:, None] == lower_rows[None, :], axis=1)
    owned = live & jnp.logical_not(in_lower & has_below)
    weighted = jnp.where(owned[:, None], filtered, 0.0)
    partial_value = lax.dot_general(
        weighted,
        weighted,
        (((0,), (0,)), ((), ())),
        precision=lax.Precision.HIGHEST,
        preferred_element_type=jnp.float32,
    )
    gram = lax.psum(partial_value, "mesh")
    total = (jnp.sum(node_counts) - shared * (devices - 1)).astype(jnp.float32)
    gram = gram / total
    factor = jnp.linalg.cholesky(gram)
    inverse = jax.scipy.linalg.solve_triangular(
        factor, jnp.eye(width, dtype=jnp.float32), lower=True
    )
    rotated = jnp.dot(
        filtered, inverse.T, precision=lax.Precision.HIGHEST, preferred_element_type=jnp.float32
    )
    return jnp.where(live[:, None], rotated, 0.0)


def solution(mesh):
    in_specs = (
        P("mesh", None),
        P("mesh"),
        P("mesh", None, None),
        P("mesh", None),
        P("mesh"),
        P(),
        P("mesh", None, None),
    )
    out_specs = P("mesh", None)
    return jax.shard_map(body, mesh=mesh, in_specs=in_specs, out_specs=out_specs, check_vma=False)
```

profile of v0, /device:TPU:0, one launch (start us, length us, event | category | flops | bytes accessed | tf_op | source)
XLA Modules:
  0.0 1117.1 jit_solution(17529059180484307456)
XLA Ops:
  49.4 75.4 %while.49 = (s32[]{:T(128)}, f32[6144,256]{1,0:T(8,128)}, pred[16]{0:T(512)(128)(4,1)S(1)}, s32[16,512]{1,0:T(8,128)}, bf16[16,512,512]{2,1,0:T(8,128)(2,1)}, /*index=5*/bf16[6144,256]{1,0:T(8,128)(2,1)S(1)}, s32[]{:T(128)}) while((s32[]{:T(128)}, f32[6144,256]{1,0:T(8,128)}, pred[16]{0:T(512)(128)(4,1)S(1)}, s32[16,512]{1,0:T(8,128)}, ...), condition=%wide.region_6.7_spmd, body=%wide.region_2.6_spmd.sunk | while | flops 134351360 | bytes 3422386 | solution.py:52
  50.7 13.8 %conditional.6 = (f32[6144,256]{1,0:T(8,128)}) conditional(s32[]{:T(128)} %bitcast.62, f32[6144,256]{1,0:T(8,128)} %get-tuple-element.664, (s32[16,512]{1,0:T(8,128)}, s32[]{:T(128)}, bf16[16,512,512]{2,1,0:T(8,128)(2,1)}, bf16[6144,256]{1,0:T(8,128)(2,1)S(1)}, f32[6144,256]{1,0:T(8,128)}) %tuple.128), branch_computations={%region_3.3_spmd, %region_4.5_spmd} | conditional | flops 134351360 | bytes 3422258 | solution.py:50
  65.7 13.8 %conditional.6 = (f32[6144,256]{1,0:T(8,128)}) conditional(s32[]{:T(128)} %bitcast.62, f32[6144,256]{1,0:T(8,128)} %get-tuple-element.664, (s32[16,512]{1,0:T(8,128)}, s32[]{:T(128)}, bf16[16,512,512]{2,1,0:T(8,128)(2,1)}, bf16[6144,256]{1,0:T(8,128)(2,1)S(1)}, f32[6144,256]{1,0:T(8,128)}) %tuple.128), branch_computations={%region_3.3_spmd, %region_4.5_spmd} | conditional | flops 134351360 | bytes 3422258 | solution.py:50
  80.7 13.8 %conditional.6 = (f32[6144,256]{1,0:T(8,128)}) conditional(s32[]{:T(128)} %bitcast.62, f32[6144,256]{1,0:T(8,128)} %get-tuple-element.664, (s32[16,512]{1,0:T(8,128)}, s32[]{:T(128)}, bf16[16,512,512]{2,1,0:T(8,128)(2,1)}, bf16[6144,256]{1,0:T(8,128)(2,1)S(1)}, f32[6144,256]{1,0:T(8,128)}) %tuple.128), branch_computations={%region_3.3_spmd, %region_4.5_spmd} | conditional | flops 134351360 | bytes 3422258 | solution.py:50
  95.7 13.8 %conditional.6 = (f32[6144,256]{1,0:T(8,128)}) conditional(s32[]{:T(128)} %bitcast.62, f32[6144,256]{1,0:T(8,128)} %get-tuple-element.664, (s32[16,512]{1,0:T(8,128)}, s32[]{:T(128)}, bf16[16,512,512]{2,1,0:T(8,128)(2,1)}, bf16[6144,256]{1,0:T(8,128)(2,1)S(1)}, f32[6144,256]{1,0:T(8,128)}) %tuple.128), branch_computations={%region_3.3_spmd, %region_4.5_spmd} | conditional | flops 134351360 | bytes 3422258 | solution.py:50
  129.3 166.7 %collective-permute-start.2 = (f32[384,256]{1,0:T(8,128)S(1)}, f32[384,256]{1,0:T(8,128)S(1)}, u32[]{:S(2)}, u32[]{:S(2)}) collective-permute-start(f32[384,256]{1,0:T(8,128)S(1)} %gather_fusion.6), channel_id=1, source_target_pairs={{0,1},{1,2},{2,3},{3,4},{4,5},{5,6},{6,7},{7,8},{8,9},{9,10},{10,1... | collective-permute-start | bytes 1179656 | tf_op jit(solution)/shard_map/ppermute | solution.py:10
  326.9 75.4 %while.50 = (s32[]{:T(128)}, f32[6144,256]{1,0:T(8,128)}, pred[16]{0:T(512)(128)(4,1)S(1)}, s32[16,512]{1,0:T(8,128)}, bf16[16,512,512]{2,1,0:T(8,128)(2,1)}, /*index=5*/bf16[6144,256]{1,0:T(8,128)(2,1)S(1)}, s32[]{:T(128)}) while((s32[]{:T(128)}, f32[6144,256]{1,0:T(8,128)}, pred[16]{0:T(512)(128)(4,1)S(1)}, s32[16,512]{1,0:T(8,128)}, ...), condition=%wide.region_13.14_spmd, body=%wide.region_9.13_spmd.sunk | while | flops 134351360 | bytes 3422386 | solution.py:52
  328.1 13.8 %conditional.7 = (f32[6144,256]{1,0:T(8,128)}) conditional(s32[]{:T(128)} %bitcast.63, f32[6144,256]{1,0:T(8,128)} %get-tuple-element.685, (s32[16,512]{1,0:T(8,128)}, s32[]{:T(128)}, bf16[16,512,512]{2,1,0:T(8,128)(2,1)}, bf16[6144,256]{1,0:T(8,128)(2,1)S(1)}, f32[6144,256]{1,0:T(8,128)}) %tuple.130), branch_computations={%region_10.10_spmd, %region_11.12_spmd} | conditional | flops 134351360 | bytes 3422258 | solution.py:50
  343.1 13.8 %conditional.7 = (f32[6144,256]{1,0:T(8,128)}) conditional(s32[]{:T(128)} %bitcast.63, f32[6144,256]{1,0:T(8,128)} %get-tuple-element.685, (s32[16,512]{1,0:T(8,128)}, s32[]{:T(128)}, bf16[16,512,512]{2,1,0:T(8,128)(2,1)}, bf16[6144,256]{1,0:T(8,128)(2,1)S(1)}, f32[6144,256]{1,0:T(8,128)}) %tuple.130), branch_computations={%region_10.10_spmd, %region_11.12_spmd} | conditional | flops 134351360 | bytes 3422258 | solution.py:50
  358.1 13.8 %conditional.7 = (f32[6144,256]{1,0:T(8,128)}) conditional(s32[]{:T(128)} %bitcast.63, f32[6144,256]{1,0:T(8,128)} %get-tuple-element.685, (s32[16,512]{1,0:T(8,128)}, s32[]{:T(128)}, bf16[16,512,512]{2,1,0:T(8,128)(2,1)}, bf16[6144,256]{1,0:T(8,128)(2,1)S(1)}, f32[6144,256]{1,0:T(8,128)}) %tuple.130), branch_computations={%region_10.10_spmd, %region_11.12_spmd} | conditional | flops 134351360 | bytes 3422258 | solution.py:50
  373.1 13.8 %conditional.7 = (f32[6144,256]{1,0:T(8,128)}) conditional(s32[]{:T(128)} %bitcast.63, f32[6144,256]{1,0:T(8,128)} %get-tuple-element.685, (s32[16,512]{1,0:T(8,128)}, s32[]{:T(128)}, bf16[16,512,512]{2,1,0:T(8,128)(2,1)}, bf16[6144,256]{1,0:T(8,128)(2,1)S(1)}, f32[6144,256]{1,0:T(8,128)}) %tuple.130), branch_computations={%region_10.10_spmd, %region_11.12_spmd} | conditional | flops 134351360 | bytes 3422258 | solution.py:50
  406.8 167.9 %collective-permute-start.4 = (f32[384,256]{1,0:T(8,128)S(1)}, f32[384,256]{1,0:T(8,128)S(1)}, u32[]{:S(2)}, u32[]{:S(2)}) collective-permute-start(f32[384,256]{1,0:T(8,128)S(1)} %gather_fusion.8), channel_id=1, source_target_pairs={{0,1},{1,2},{2,3},{3,4},{4,5},{5,6},{6,7},{7,8},{8,9},{9,10},{10,1... | collective-permute-start | bytes 1179656 | tf_op jit(solution)/shard_map/ppermute | solution.py:10
  606.9 75.5 %while.51 = (s32[]{:T(128)}, f32[6144,256]{1,0:T(8,128)}, pred[16]{0:T(512)(128)(4,1)S(1)}, s32[16,512]{1,0:T(8,128)}, bf16[16,512,512]{2,1,0:T(8,128)(2,1)}, /*index=5*/bf16[6144,256]{1,0:T(8,128)(2,1)S(1)}, s32[]{:T(128)}) while((s32[]{:T(128)}, f32[6144,256]{1,0:T(8,128)}, pred[16]{0:T(512)(128)(4,1)S(1)}, s32[16,512]{1,0:T(8,128)}, ...), condition=%wide.region_20.21_spmd, body=%wide.region_16.20_spmd.sunk | while | flops 134351360 | bytes 3422386 | solution.py:52
  608.1 13.8 %conditional.8 = (f32[6144,256]{1,0:T(8,128)}) conditional(s32[]{:T(128)} %bitcast.64, f32[6144,256]{1,0:T(8,128)} %get-tuple-element.706, (s32[16,512]{1,0:T(8,128)}, s32[]{:T(128)}, bf16[16,512,512]{2,1,0:T(8,128)(2,1)}, bf16[6144,256]{1,0:T(8,128)(2,1)S(1)}, f32[6144,256]{1,0:T(8,128)}) %tuple.132), branch_computations={%region_17.17_spmd, %region_18.19_spmd} | conditional | flops 134351360 | bytes 3422258 | solution.py:50
  623.2 13.8 %conditional.8 = (f32[6144,256]{1,0:T(8,128)}) conditional(s32[]{:T(128)} %bitcast.64, f32[6144,256]{1,0:T(8,128)} %get-tuple-element.706, (s32[16,512]{1,0:T(8,128)}, s32[]{:T(128)}, bf16[16,512,512]{2,1,0:T(8,128)(2,1)}, bf16[6144,256]{1,0:T(8,128)(2,1)S(1)}, f32[6144,256]{1,0:T(8,128)}) %tuple.132), branch_computations={%region_17.17_spmd, %region_18.19_spmd} | conditional | flops 134351360 | bytes 3422258 | solution.py:50
  638.2 13.8 %conditional.8 = (f32[6144,256]{1,0:T(8,128)}) conditional(s32[]{:T(128)} %bitcast.64, f32[6144,256]{1,0:T(8,128)} %get-tuple-element.706, (s32[16,512]{1,0:T(8,128)}, s32[]{:T(128)}, bf16[16,512,512]{2,1,0:T(8,128)(2,1)}, bf16[6144,256]{1,0:T(8,128)(2,1)S(1)}, f32[6144,256]{1,0:T(8,128)}) %tuple.132), branch_computations={%region_17.17_spmd, %region_18.19_spmd} | conditional | flops 134351360 | bytes 3422258 | solution.py:50
  653.3 13.8 %conditional.8 = (f32[6144,256]{1,0:T(8,128)}) conditional(s32[]{:T(128)} %bitcast.64, f32[6144,256]{1,0:T(8,128)} %get-tuple-element.706, (s32[16,512]{1,0:T(8,128)}, s32[]{:T(128)}, bf16[16,512,512]{2,1,0:T(8,128)(2,1)}, bf16[6144,256]{1,0:T(8,128)(2,1)S(1)}, f32[6144,256]{1,0:T(8,128)}) %tuple.132), branch_computations={%region_17.17_spmd, %region_18.19_spmd} | conditional | flops 134351360 | bytes 3422258 | solution.py:50
  691.4 168.4 %collective-permute-start.6 = (f32[384,256]{1,0:T(8,128)S(1)}, f32[384,256]{1,0:T(8,128)S(1)}, u32[]{:S(2)}, u32[]{:S(2)}) collective-permute-start(f32[384,256]{1,0:T(8,128)S(1)} %gather_fusion.10), channel_id=1, source_target_pairs={{0,1},{1,2},{2,3},{3,4},{4,5},{5,6},{6,7},{7,8},{8,9},{9,10},{10,1... | collective-permute-start | bytes 1179656 | tf_op jit(solution)/shard_map/ppermute | solution.py:10
  892.0 12.9 %fusion.13 = f32[256,256]{0,1:T(8,128)} fusion(f32[6144,256]{1,0:T(8,128)S(1)} %multiply_subtract_fusion, pred[6144]{0:T(1024)(128)(4,1)S(1)} %not_and_fusion), kind=kOutput, calls=%fused_computation.47 | convolution fusion | flops 4833411072 | bytes 6559744 | tf_op jit(solution)/shard_map/dot_general | solution.py:67
  906.2 132.1 %all-reduce.3.cloned.1.call-done = f32[256,256]{0,1:T(8,128)} async-done(((f32[256,256]{0,1:T(8,128)}), f32[256,256]{0,1:T(8,128)}) %all-reduce.3.cloned.1.call-update) | async-done | bytes 262160 | tf_op jit(solution)/shard_map/psum | solution.py:74
  1040.8 11.7 %cholesky.50 = f32[128,128]{1,0:T(8,128)S(1)} custom-call(f32[128,128]{1,0:T(8,128)S(1)} %cholesky.118), custom_call_target="Cholesky" | custom-call | tf_op jit(solution)/shard_map/jit(cholesky)/cholesky | solution.py:77
  1052.6 9.8 custom-call.15
  1062.8 11.7 %cholesky.105 = f32[128,128]{1,0:T(8,128)S(1)} custom-call(f32[128,128]{1,0:T(8,128)S(1)} %convolution_subtract_fusion.1), custom_call_target="Cholesky" | custom-call | tf_op jit(solution)/shard_map/jit(cholesky)/cholesky | solution.py:77
  1080.4 19.8 %custom-call.16 = f32[2,128,128]{1,2,0:T(8,128)S(1)} custom-call(f32[2,128,128]{2,1,0:T(8,128)S(1)} %get-tuple-element.459), custom_call_target="InvertDiagBlocksLowerTriangular" | custom-call | tf_op jit(solution)/shard_map/jit(_solve_triangular)/triangular_solve | solution.py:78
  (229 shorter events, 371.4 us)
Async XLA Ops:
  6.5 1031.7 %all-reduce.3.cloned.1.call-start = ((), (), s32[]{:S(2)}) async-start(), calls=%async_computation | async-start | bytes 524288 | tf_op jit(solution)/shard_map/psum | solution.py:74
  7.3 5.8 copy-start.1
  15.7 14.6 %collective-permute-start = (f32[384]{0:T(512)S(1)}, f32[384]{0:T(512)S(1)}, u32[]{:S(2)}, u32[]{:S(2)}) collective-permute-start(f32[384]{0:T(512)S(1)} %gather_fusion.3), channel_id=1, source_target_pairs={{0,1},{1,2},{2,3},{3,4},{4,5},{5,6},{6,7},{7,8},{8,9},{9,10},{10,1... | collective-permute-start | bytes 4616 | tf_op jit(solution)/shard_map/ppermute | solution.py:10
  22.5 10.8 collective-permute-start.1
  129.3 173.0 %collective-permute-start.2 = (f32[384,256]{1,0:T(8,128)S(1)}, f32[384,256]{1,0:T(8,128)S(1)}, u32[]{:S(2)}, u32[]{:S(2)}) collective-permute-start(f32[384,256]{1,0:T(8,128)S(1)} %gather_fusion.6), channel_id=1, source_target_pairs={{0,1},{1,2},{2,3},{3,4},{4,5},{5,6},{6,7},{7,8},{8,9},{9,10},{10,1... | collective-permute-start | bytes 1179656 | tf_op jit(solution)/shard_map/ppermute | solution.py:10
  300.5 9.6 collective-permute-start.3
  406.8 173.7 %collective-permute-start.4 = (f32[384,256]{1,0:T(8,128)S(1)}, f32[384,256]{1,0:T(8,128)S(1)}, u32[]{:S(2)}, u32[]{:S(2)}) collective-permute-start(f32[384,256]{1,0:T(8,128)S(1)} %gather_fusion.8), channel_id=1, source_target_pairs={{0,1},{1,2},{2,3},{3,4},{4,5},{5,6},{6,7},{7,8},{8,9},{9,10},{10,1... | collective-permute-start | bytes 1179656 | tf_op jit(solution)/shard_map/ppermute | solution.py:10
  579.1 9.3 collective-permute-start.5
  682.4 179.5 %copy-start.2 = (s32[32]{0:T(128)S(1)}, s32[32]{0:T(128)}, u32[]{:S(2)}) copy-start(s32[32]{0:T(128)} %param.24) | copy-start | bytes 388
  691.4 172.4 %collective-permute-start.6 = (f32[384,256]{1,0:T(8,128)S(1)}, f32[384,256]{1,0:T(8,128)S(1)}, u32[]{:S(2)}, u32[]{:S(2)}) collective-permute-start(f32[384,256]{1,0:T(8,128)S(1)} %gather_fusion.10), channel_id=1, source_target_pairs={{0,1},{1,2},{2,3},{3,4},{4,5},{5,6},{6,7},{7,8},{8,9},{9,10},{10,1... | collective-permute-start | bytes 1179656 | tf_op jit(solution)/shard_map/ppermute | solution.py:10
  859.7 12.0 %collective-permute-start.7 = (f32[384,256]{1,0:T(8,128)S(1)}, f32[384,256]{1,0:T(8,128)S(1)}, u32[]{:S(2)}, u32[]{:S(2)}) collective-permute-start(f32[384,256]{1,0:T(8,128)S(1)} %gather_fusion.11), channel_id=1, source_target_pairs={{1,0},{2,1},{3,2},{4,3},{5,4},{6,5},{7,6},{8,7},{9,8},{10,9},{11,1... | collective-permute-start | bytes 1179656 | tf_op jit(solution)/shard_map/ppermute | solution.py:10
  889.3 2.7 copy-start
Sparse Core Ops, SparseCore 0:
  905.0 133.2 all-reduce.2
where the time goes:
time: 1140 us; the launch traced here: 1120 us
  starting transfers between devices  514 us (45%)
  other arithmetic  258 us (23%)
  waiting for transfers between devices  132 us (12%)
  local copies, waits for them, and re-layouts  115 us (10%)
  matrix products  48.7 us (4%)
  loops' own time  32.5 us (3%)
  between operations  16.5 us (1%)
    ppermute x8, starting transfers between devices, passed_along(): return lax.ppermute(block, axis, route)  514 us
    psum x1, waiting for transfers between devices, body(): gram = lax.psum(partial_value, 'mesh')  132 us
    scatter-add x12, other arithmetic, compute(): return acc.at[rows].add(part)  107 us
    scatter-add x6, other arithmetic, ham(): local.at[lower_rows].add(coming_up).at[upper_rows].add(coming_down)  47.2 us
    another operation x6, other arithmetic, body(): factor = jnp.linalg.cholesky(gram)  34 us
    another operation x3, loops' own time, ham(): local = lax.fori_loop(0, slots, add_element, empty)  31.5 us
    dynamic_slice x48, local copies, waits for them, and re-layouts, add_element(): return lax.cond(slot_live[slot], compute, lambda acc: acc, total)  28.8 us
    dot_general x12, matrix products, compute(): jnp.dot(element_blocks[slot], scaled[rows], preferred_element_type=jnp.fl...  25.6 us
  transfers between devices with their start and end apart: 9, of which 1 were waited for; matrix products, arithmetic and copies ran while one was open for 4% of the time, Pallas kernels for 0%

commit v1 on v0

--- a/solution.py
+++ b/solution.py
@@ -71,7 +71,7 @@
         precision=lax.Precision.HIGHEST,
         preferred_element_type=jnp.float32,
     )
-    gram = lax.psum(partial_value, "mesh")
+    gram = jnp.sum(lax.all_gather(partial_value, "mesh"), axis=0)
     total = (jnp.sum(node_counts) - shared * (devices - 1)).astype(jnp.float32)
     gram = gram / total
     factor = jnp.linalg.cholesky(gram)

time: 1140 us -> 1090 us (0.956)
  waiting for transfers between devices: 132 us -> 83.2 us
    psum x1 -> x0, waiting for transfers between devices: 132 us -> none  [body(): gram = lax.psum(partial_value, 'mesh')]
    all_gather x0 -> x1, waiting for transfers between devices: none -> 83.1 us  [body(): gram = jnp.sum(lax.all_gather(partial_value, 'mesh'), axis=0)]
where the time goes in v1:
time: 1090 us; the launch traced here: 1070 us
  starting transfers between devices  514 us (47%)
  other arithmetic  261 us (24%)
  local copies, waits for them, and re-layouts  115 us (11%)
  waiting for transfers between devices  83.2 us (8%)
  matrix products  48.3 us (4%)
  loops' own time  32.5 us (3%)
  between operations  16.9 us (2%)
    ppermute x8, starting transfers between devices, passed_along(): return lax.ppermute(block, axis, route)  514 us
    scatter-add x12, other arithmetic, compute(): return acc.at[rows].add(part)  107 us
    all_gather x1, waiting for transfers between devices, body(): gram = jnp.sum(lax.all_gather(partial_value, 'mesh'), axis=0)  83.1 us
    scatter-add x6, other arithmetic, ham(): local.at[lower_rows].add(coming_up).at[upper_rows].add(coming_down)  47.4 us
    another operation x6, other arithmetic, body(): factor = jnp.linalg.cholesky(gram)  34 us
    another operation x3, loops' own time, ham(): local = lax.fori_loop(0, slots, add_element, empty)  31.5 us
    dynamic_slice x48, local copies, waits for them, and re-layouts, add_element(): return lax.cond(slot_live[slot], compute, lambda acc: acc, total)  28.8 us
    dot_general x12, matrix products, compute(): jnp.dot(element_blocks[slot], scaled[rows], preferred_element_type=jnp.fl...  25.6 us
  transfers between devices with their start and end apart: 9, of which 1 were waited for; matrix products, arithmetic and copies ran while one was open for 4% of the time, Pallas kernels for 0%

profile of v1, /device:TPU:0, one launch (start us, length us, event | category | flops | bytes accessed | tf_op | source)
XLA Modules:
  0.0 1070.3 jit_solution(3935579334490655620)
XLA Ops:
  49.4 75.4 %while.49 = (s32[]{:T(128)}, f32[6144,256]{1,0:T(8,128)}, pred[16]{0:T(512)(128)(4,1)S(1)}, s32[16,512]{1,0:T(8,128)}, bf16[16,512,512]{2,1,0:T(8,128)(2,1)}, /*index=5*/bf16[6144,256]{1,0:T(8,128)(2,1)S(1)}, s32[]{:T(128)}) while((s32[]{:T(128)}, f32[6144,256]{1,0:T(8,128)}, pred[16]{0:T(512)(128)(4,1)S(1)}, s32[16,512]{1,0:T(8,128)}, ...), condition=%wide.region_6.7_spmd, body=%wide.region_2.6_spmd.sunk | while | flops 134351360 | bytes 3422386 | solution.py:52
  50.7 13.8 %conditional.6 = (f32[6144,256]{1,0:T(8,128)}) conditional(s32[]{:T(128)} %bitcast.63, f32[6144,256]{1,0:T(8,128)} %get-tuple-element.664, (s32[16,512]{1,0:T(8,128)}, s32[]{:T(128)}, bf16[16,512,512]{2,1,0:T(8,128)(2,1)}, bf16[6144,256]{1,0:T(8,128)(2,1)S(1)}, f32[6144,256]{1,0:T(8,128)}) %tuple.128), branch_computations={%region_3.3_spmd, %region_4.5_spmd} | conditional | flops 134351360 | bytes 3422258 | solution.py:50
  65.7 13.8 %conditional.6 = (f32[6144,256]{1,0:T(8,128)}) conditional(s32[]{:T(128)} %bitcast.63, f32[6144,256]{1,0:T(8,128)} %get-tuple-element.664, (s32[16,512]{1,0:T(8,128)}, s32[]{:T(128)}, bf16[16,512,512]{2,1,0:T(8,128)(2,1)}, bf16[6144,256]{1,0:T(8,128)(2,1)S(1)}, f32[6144,256]{1,0:T(8,128)}) %tuple.128), branch_computations={%region_3.3_spmd, %region_4.5_spmd} | conditional | flops 134351360 | bytes 3422258 | solution.py:50
  80.7 13.8 %conditional.6 = (f32[6144,256]{1,0:T(8,128)}) conditional(s32[]{:T(128)} %bitcast.63, f32[6144,256]{1,0:T(8,128)} %get-tuple-element.664, (s32[16,512]{1,0:T(8,128)}, s32[]{:T(128)}, bf16[16,512,512]{2,1,0:T(8,128)(2,1)}, bf16[6144,256]{1,0:T(8,128)(2,1)S(1)}, f32[6144,256]{1,0:T(8,128)}) %tuple.128), branch_computations={%region_3.3_spmd, %region_4.5_spmd} | conditional | flops 134351360 | bytes 3422258 | solution.py:50
  95.7 13.8 %conditional.6 = (f32[6144,256]{1,0:T(8,128)}) conditional(s32[]{:T(128)} %bitcast.63, f32[6144,256]{1,0:T(8,128)} %get-tuple-element.664, (s32[16,512]{1,0:T(8,128)}, s32[]{:T(128)}, bf16[16,512,512]{2,1,0:T(8,128)(2,1)}, bf16[6144,256]{1,0:T(8,128)(2,1)S(1)}, f32[6144,256]{1,0:T(8,128)}) %tuple.128), branch_computations={%region_3.3_spmd, %region_4.5_spmd} | conditional | flops 134351360 | bytes 3422258 | solution.py:50
  129.3 166.7 %collective-permute-start.2 = (f32[384,256]{1,0:T(8,128)S(1)}, f32[384,256]{1,0:T(8,128)S(1)}, u32[]{:S(2)}, u32[]{:S(2)}) collective-permute-start(f32[384,256]{1,0:T(8,128)S(1)} %gather_fusion.6), channel_id=1, source_target_pairs={{0,1},{1,2},{2,3},{3,4},{4,5},{5,6},{6,7},{7,8},{8,9},{9,10},{10,1... | collective-permute-start | bytes 1179656 | tf_op jit(solution)/shard_map/ppermute | solution.py:10
  326.6 75.4 %while.50 = (s32[]{:T(128)}, f32[6144,256]{1,0:T(8,128)}, pred[16]{0:T(512)(128)(4,1)S(1)}, s32[16,512]{1,0:T(8,128)}, bf16[16,512,512]{2,1,0:T(8,128)(2,1)}, /*index=5*/bf16[6144,256]{1,0:T(8,128)(2,1)S(1)}, s32[]{:T(128)}) while((s32[]{:T(128)}, f32[6144,256]{1,0:T(8,128)}, pred[16]{0:T(512)(128)(4,1)S(1)}, s32[16,512]{1,0:T(8,128)}, ...), condition=%wide.region_13.14_spmd, body=%wide.region_9.13_spmd.sunk | while | flops 134351360 | bytes 3422386 | solution.py:52
  327.8 13.8 %conditional.7 = (f32[6144,256]{1,0:T(8,128)}) conditional(s32[]{:T(128)} %bitcast.64, f32[6144,256]{1,0:T(8,128)} %get-tuple-element.685, (s32[16,512]{1,0:T(8,128)}, s32[]{:T(128)}, bf16[16,512,512]{2,1,0:T(8,128)(2,1)}, bf16[6144,256]{1,0:T(8,128)(2,1)S(1)}, f32[6144,256]{1,0:T(8,128)}) %tuple.130), branch_computations={%region_10.10_spmd, %region_11.12_spmd} | conditional | flops 134351360 | bytes 3422258 | solution.py:50
  342.8 13.8 %conditional.7 = (f32[6144,256]{1,0:T(8,128)}) conditional(s32[]{:T(128)} %bitcast.64, f32[6144,256]{1,0:T(8,128)} %get-tuple-element.685, (s32[16,512]{1,0:T(8,128)}, s32[]{:T(128)}, bf16[16,512,512]{2,1,0:T(8,128)(2,1)}, bf16[6144,256]{1,0:T(8,128)(2,1)S(1)}, f32[6144,256]{1,0:T(8,128)}) %tuple.130), branch_computations={%region_10.10_spmd, %region_11.12_spmd} | conditional | flops 134351360 | bytes 3422258 | solution.py:50
  357.8 13.8 %conditional.7 = (f32[6144,256]{1,0:T(8,128)}) conditional(s32[]{:T(128)} %bitcast.64, f32[6144,256]{1,0:T(8,128)} %get-tuple-element.685, (s32[16,512]{1,0:T(8,128)}, s32[]{:T(128)}, bf16[16,512,512]{2,1,0:T(8,128)(2,1)}, bf16[6144,256]{1,0:T(8,128)(2,1)S(1)}, f32[6144,256]{1,0:T(8,128)}) %tuple.130), branch_computations={%region_10.10_spmd, %region_11.12_spmd} | conditional | flops 134351360 | bytes 3422258 | solution.py:50
  372.9 13.8 %conditional.7 = (f32[6144,256]{1,0:T(8,128)}) conditional(s32[]{:T(128)} %bitcast.64, f32[6144,256]{1,0:T(8,128)} %get-tuple-element.685, (s32[16,512]{1,0:T(8,128)}, s32[]{:T(128)}, bf16[16,512,512]{2,1,0:T(8,128)(2,1)}, bf16[6144,256]{1,0:T(8,128)(2,1)S(1)}, f32[6144,256]{1,0:T(8,128)}) %tuple.130), branch_computations={%region_10.10_spmd, %region_11.12_spmd} | conditional | flops 134351360 | bytes 3422258 | solution.py:50
  406.5 167.9 %collective-permute-start.4 = (f32[384,256]{1,0:T(8,128)S(1)}, f32[384,256]{1,0:T(8,128)S(1)}, u32[]{:S(2)}, u32[]{:S(2)}) collective-permute-start(f32[384,256]{1,0:T(8,128)S(1)} %gather_fusion.8), channel_id=1, source_target_pairs={{0,1},{1,2},{2,3},{3,4},{4,5},{5,6},{6,7},{7,8},{8,9},{9,10},{10,1... | collective-permute-start | bytes 1179656 | tf_op jit(solution)/shard_map/ppermute | solution.py:10
  607.5 75.5 %while.51 = (s32[]{:T(128)}, f32[6144,256]{1,0:T(8,128)}, pred[16]{0:T(512)(128)(4,1)S(1)}, s32[16,512]{1,0:T(8,128)}, bf16[16,512,512]{2,1,0:T(8,128)(2,1)}, /*index=5*/bf16[6144,256]{1,0:T(8,128)(2,1)S(1)}, s32[]{:T(128)}) while((s32[]{:T(128)}, f32[6144,256]{1,0:T(8,128)}, pred[16]{0:T(512)(128)(4,1)S(1)}, s32[16,512]{1,0:T(8,128)}, ...), condition=%wide.region_20.21_spmd, body=%wide.region_16.20_spmd.sunk | while | flops 134351360 | bytes 3422386 | solution.py:52
  608.7 13.8 %conditional.8 = (f32[6144,256]{1,0:T(8,128)}) conditional(s32[]{:T(128)} %bitcast.65, f32[6144,256]{1,0:T(8,128)} %get-tuple-element.706, (s32[16,512]{1,0:T(8,128)}, s32[]{:T(128)}, bf16[16,512,512]{2,1,0:T(8,128)(2,1)}, bf16[6144,256]{1,0:T(8,128)(2,1)S(1)}, f32[6144,256]{1,0:T(8,128)}) %tuple.132), branch_computations={%region_17.17_spmd, %region_18.19_spmd} | conditional | flops 134351360 | bytes 3422258 | solution.py:50
  623.7 13.8 %conditional.8 = (f32[6144,256]{1,0:T(8,128)}) conditional(s32[]{:T(128)} %bitcast.65, f32[6144,256]{1,0:T(8,128)} %get-tuple-element.706, (s32[16,512]{1,0:T(8,128)}, s32[]{:T(128)}, bf16[16,512,512]{2,1,0:T(8,128)(2,1)}, bf16[6144,256]{1,0:T(8,128)(2,1)S(1)}, f32[6144,256]{1,0:T(8,128)}) %tuple.132), branch_computations={%region_17.17_spmd, %region_18.19_spmd} | conditional | flops 134351360 | bytes 3422258 | solution.py:50
  638.8 13.8 %conditional.8 = (f32[6144,256]{1,0:T(8,128)}) conditional(s32[]{:T(128)} %bitcast.65, f32[6144,256]{1,0:T(8,128)} %get-tuple-element.706, (s32[16,512]{1,0:T(8,128)}, s32[]{:T(128)}, bf16[16,512,512]{2,1,0:T(8,128)(2,1)}, bf16[6144,256]{1,0:T(8,128)(2,1)S(1)}, f32[6144,256]{1,0:T(8,128)}) %tuple.132), branch_computations={%region_17.17_spmd, %region_18.19_spmd} | conditional | flops 134351360 | bytes 3422258 | solution.py:50
  653.8 13.8 %conditional.8 = (f32[6144,256]{1,0:T(8,128)}) conditional(s32[]{:T(128)} %bitcast.65, f32[6144,256]{1,0:T(8,128)} %get-tuple-element.706, (s32[16,512]{1,0:T(8,128)}, s32[]{:T(128)}, bf16[16,512,512]{2,1,0:T(8,128)(2,1)}, bf16[6144,256]{1,0:T(8,128)(2,1)S(1)}, f32[6144,256]{1,0:T(8,128)}) %tuple.132), branch_computations={%region_17.17_spmd, %region_18.19_spmd} | conditional | flops 134351360 | bytes 3422258 | solution.py:50
  691.9 168.4 %collective-permute-start.6 = (f32[384,256]{1,0:T(8,128)S(1)}, f32[384,256]{1,0:T(8,128)S(1)}, u32[]{:S(2)}, u32[]{:S(2)}) collective-permute-start(f32[384,256]{1,0:T(8,128)S(1)} %gather_fusion.10), channel_id=1, source_target_pairs={{0,1},{1,2},{2,3},{3,4},{4,5},{5,6},{6,7},{7,8},{8,9},{9,10},{10,1... | collective-permute-start | bytes 1179656 | tf_op jit(solution)/shard_map/ppermute | solution.py:10
  891.3 12.5 %fusion.13 = f32[256,256]{1,0:T(8,128)} fusion(f32[6144,256]{1,0:T(8,128)S(1)} %multiply_subtract_fusion, pred[6144]{0:T(1024)(128)(4,1)S(1)} %not_and_fusion), kind=kOutput, calls=%fused_computation.47 | convolution fusion | flops 4833411072 | bytes 6559744 | tf_op jit(solution)/shard_map/dot_general | solution.py:67
  905.8 83.1 %all-gather.3.cloned.1.call-done = f32[8192,256]{1,0:T(8,128)} async-done(((f32[256,256]{1,0:T(8,128)}), f32[8192,256]{1,0:T(8,128)}) %all-gather.3.cloned.1.call-update) | async-done | bytes 8388624 | tf_op jit(solution)/shard_map/all_gather | solution.py:74
  993.4 11.7 %cholesky.50 = f32[128,128]{1,0:T(8,128)S(1)} custom-call(f32[128,128]{1,0:T(8,128)S(1)} %cholesky.118), custom_call_target="Cholesky" | custom-call | tf_op jit(solution)/shard_map/jit(cholesky)/cholesky | solution.py:77
  1005.2 9.8 custom-call.15
  1015.5 11.7 %cholesky.105 = f32[128,128]{1,0:T(8,128)S(1)} custom-call(f32[128,128]{1,0:T(8,128)S(1)} %convolution_subtract_fusion.1), custom_call_target="Cholesky" | custom-call | tf_op jit(solution)/shard_map/jit(cholesky)/cholesky | solution.py:77
  1033.3 19.9 %custom-call.16 = f32[2,128,128]{1,2,0:T(8,128)S(1)} custom-call(f32[2,128,128]{2,1,0:T(8,128)S(1)} %get-tuple-element.459), custom_call_target="InvertDiagBlocksLowerTriangular" | custom-call | tf_op jit(solution)/shard_map/jit(_solve_triangular)/triangular_solve | solution.py:78
  (231 shorter events, 373.6 us)
Async XLA Ops:
  6.5 982.4 %all-gather.3.cloned.1.call-start = ((), (), s32[]{:S(2)}) async-start(), calls=%async_computation | async-start | bytes 8650752 | tf_op jit(solution)/shard_map/all_gather | solution.py:74
  7.3 5.8 copy-start.1
  15.7 14.6 %collective-permute-start = (f32[384]{0:T(512)S(1)}, f32[384]{0:T(512)S(1)}, u32[]{:S(2)}, u32[]{:S(2)}) collective-permute-start(f32[384]{0:T(512)S(1)} %gather_fusion.3), channel_id=1, source_target_pairs={{0,1},{1,2},{2,3},{3,4},{4,5},{5,6},{6,7},{7,8},{8,9},{9,10},{10,1... | collective-permute-start | bytes 4616 | tf_op jit(solution)/shard_map/ppermute | solution.py:10
  22.5 10.8 %collective-permute-start.1 = (f32[384,256]{1,0:T(8,128)S(1)}, f32[384,256]{1,0:T(8,128)S(1)}, u32[]{:S(2)}, u32[]{:S(2)}) collective-permute-start(f32[384,256]{1,0:T(8,128)S(1)} %gather_fusion.5), channel_id=1, source_target_pairs={{0,1},{1,2},{2,3},{3,4},{4,5},{5,6},{6,7},{7,8},{8,9},{9,10},{10,1... | collective-permute-start | bytes 1179656 | tf_op jit(solution)/shard_map/ppermute | solution.py:10
  129.3 172.7 %collective-permute-start.2 = (f32[384,256]{1,0:T(8,128)S(1)}, f32[384,256]{1,0:T(8,128)S(1)}, u32[]{:S(2)}, u32[]{:S(2)}) collective-permute-start(f32[384,256]{1,0:T(8,128)S(1)} %gather_fusion.6), channel_id=1, source_target_pairs={{0,1},{1,2},{2,3},{3,4},{4,5},{5,6},{6,7},{7,8},{8,9},{9,10},{10,1... | collective-permute-start | bytes 1179656 | tf_op jit(solution)/shard_map/ppermute | solution.py:10
  300.5 9.3 collective-permute-start.3
  402.0 178.2 %copy-start.2 = (s32[32]{0:T(128)S(1)}, s32[32]{0:T(128)}, u32[]{:S(2)}) copy-start(s32[32]{0:T(128)} %param.24) | copy-start | bytes 388
  406.5 174.3 %collective-permute-start.4 = (f32[384,256]{1,0:T(8,128)S(1)}, f32[384,256]{1,0:T(8,128)S(1)}, u32[]{:S(2)}, u32[]{:S(2)}) collective-permute-start(f32[384,256]{1,0:T(8,128)S(1)} %gather_fusion.8), channel_id=1, source_target_pairs={{0,1},{1,2},{2,3},{3,4},{4,5},{5,6},{6,7},{7,8},{8,9},{9,10},{10,1... | collective-permute-start | bytes 1179656 | tf_op jit(solution)/shard_map/ppermute | solution.py:10
  578.9 10.2 collective-permute-start.5
  691.9 171.2 %collective-permute-start.6 = (f32[384,256]{1,0:T(8,128)S(1)}, f32[384,256]{1,0:T(8,128)S(1)}, u32[]{:S(2)}, u32[]{:S(2)}) collective-permute-start(f32[384,256]{1,0:T(8,128)S(1)} %gather_fusion.10), channel_id=1, source_target_pairs={{0,1},{1,2},{2,3},{3,4},{4,5},{5,6},{6,7},{7,8},{8,9},{9,10},{10,1... | collective-permute-start | bytes 1179656 | tf_op jit(solution)/shard_map/ppermute | solution.py:10
  860.3 10.7 %collective-permute-start.7 = (f32[384,256]{1,0:T(8,128)S(1)}, f32[384,256]{1,0:T(8,128)S(1)}, u32[]{:S(2)}, u32[]{:S(2)}) collective-permute-start(f32[384,256]{1,0:T(8,128)S(1)} %gather_fusion.11), channel_id=1, source_target_pairs={{1,0},{2,1},{3,2},{4,3},{5,4},{6,5},{7,6},{8,7},{9,8},{10,9},{11,1... | collective-permute-start | bytes 1179656 | tf_op jit(solution)/shard_map/ppermute | solution.py:10
  888.6 2.7 copy-start
Sparse Core Ops, SparseCore 0:
  903.9 84.9 all-gather.2
